TPU v7x, 32 devices: a whole 2x2x4 slice. The times are simulated.
32 devices in a mesh: dp: 8 (over z, y), bfly: 4 (over x, core).
Axes of the slice: x: 2, y: 2, z: 4, core: 2. Of those that a mesh axis runs over, the one named last changes fastest.
Arguments:
- tokens: bfloat16 [2048, 12288], P('dp', 'bfly'), may hold values from -6 to 6
- grad_out: bfloat16 [2048, 12288], P('dp', 'bfly'), may hold values from -6 to 6
- weight_a: bfloat16 [48, 256, 512], P('bfly', 'dp'), may hold values from -0.375 to 0.375
- weight_b: bfloat16 [96, 256, 256], P('bfly', 'dp'), may hold values from -0.375 to 0.375
- weight_c: bfloat16 [96, 256, 256], P('bfly', 'dp'), may hold values from -0.375 to 0.375
- weight_e: bfloat16 [48, 512, 256], P('bfly', 'dp'), may hold values from -0.25 to 0.25
Outputs:
- output: bfloat16 [2048, 12288], P('dp', 'bfly')
- grad_in: bfloat16 [2048, 12288], P('dp', 'bfly')
- grad_a: float32 [48, 256, 512], P('bfly', 'dp')
- grad_b: float32 [96, 256, 256], P('bfly', 'dp')
- grad_c: float32 [96, 256, 256], P('bfly', 'dp')
- grad_e: float32 [48, 512, 256], P('bfly', 'dp')
All inputs are finite; a program needn't handle non-finite values.
Results may differ from a plain program's by a relative error of at most 0.03.
Values may be sent and summed in bfloat16 or wider, within the bound.
No kernel may reach another device: no remote copies, remote signals or barrier semaphores. Data moves between devices by JAX's collectives and lax.ppermute only.
A program may use at most 128 MiB of HBM per device.

v0:
```python
import jax
import jax.numpy as jnp
from jax import lax
from jax.sharding import PartitionSpec as P

BLK = 256
gelu_scale = 0.7978845608028654


def gelu_pair(hidden):
    inner_arg = gelu_scale * (hidden + 0.044715 * hidden * hidden * hidden)
    tangent = jnp.tanh(inner_arg)
    gelu_value = 0.5 * hidden * (1.0 + tangent)
    gelu_slope = 0.5 * (1.0 + tangent) + 0.5 * hidden * (1.0 - tangent * tangent) * gelu_scale * (
        1.0 + 3.0 * 0.044715 * hidden * hidden
    )
    return (gelu_value, gelu_slope)


def regroup(parcels, group_count, after_fns):
    parcel_count = len(parcels)
    local_blocks, block_width, token_count = parcels[0].shape
    sub_width = block_width // group_count
    stacked = jnp.stack(parcels, axis=0).reshape(
        parcel_count, local_blocks, group_count, sub_width, token_count
    )
    arrived = lax.all_to_all(stacked, "bfly", split_axis=2, concat_axis=2, tiled=True)
    flat_results = []
    piece = arrived[0].reshape(local_blocks, block_width, arrived.shape[4])
    flat_results.extend(after_fns[0](piece))
    return tuple(flat_results)


def per_device(tokens, grad_out, weight_a, weight_b, weight_c, weight_e):
    group_count = lax.axis_size("bfly")
    full_a, full_b, full_c, full_e = (
        lax.all_gather(weight_a, "dp", axis=1, tiled=True),
        lax.all_gather(weight_b, "dp", axis=1, tiled=True),
        lax.all_gather(weight_c, "dp", axis=1, tiled=True),
        lax.all_gather(weight_e, "dp", axis=1, tiled=True),
    )
    token_count = tokens.shape[0]
    inner_blocks = full_a.shape[0]
    spread_width = full_a.shape[2]
    local_blocks = full_b.shape[0]
    inputs = tokens.reshape(token_count, inner_blocks, BLK).transpose(1, 2, 0)
    upstream = grad_out.reshape(token_count, inner_blocks, BLK).transpose(1, 2, 0)
    spread = jnp.einsum("kit,kio->kot", inputs, full_a, preferred_element_type=jnp.float32)
    spread = spread.astype(jnp.bfloat16).reshape(local_blocks, BLK, token_count)
    back_out = jnp.einsum("kjt,koj->kot", upstream, full_e, preferred_element_type=jnp.float32)
    back_out = back_out.astype(jnp.bfloat16).reshape(local_blocks, BLK, token_count)

    def up_second(permuted):
        return (
            permuted,
            jnp.einsum("qit,qij->qjt", permuted, full_b, preferred_element_type=jnp.float32),
        )

    def back_second(back_mid):
        return (
            back_mid,
            jnp.einsum("qjt,qij->qit", back_mid, full_c, preferred_element_type=jnp.float32),
        )

    def down_second(returned):
        wide_view = returned.reshape(inner_blocks, spread_width, returned.shape[2])
        return (
            returned,
            jnp.einsum("kot,koj->kjt", wide_view, full_e, preferred_element_type=jnp.float32),
        )

    def back_last(back_spread):
        wide_view = back_spread.reshape(inner_blocks, spread_width, back_spread.shape[2])
        return (
            back_spread,
            jnp.einsum("kot,kio->kit", wide_view, full_a, preferred_element_type=jnp.float32),
        )

    permuted, hidden = regroup((spread,), group_count, (up_second,))
    gelu_value, gelu_slope = gelu_pair(hidden)
    active = gelu_value.astype(jnp.bfloat16)
    narrowed = jnp.einsum(
        "qit,qij->qjt", active, full_c, preferred_element_type=jnp.float32
    ).astype(jnp.bfloat16)
    returned, output = regroup((narrowed,), group_count, (down_second,))
    back_mid, back_act = regroup((back_out,), group_count, (back_second,))
    back_hidden = (back_act * gelu_slope).astype(jnp.bfloat16)
    back_first = jnp.einsum(
        "qjt,qij->qit", back_hidden, full_b, preferred_element_type=jnp.float32
    ).astype(jnp.bfloat16)
    back_spread, back_input = regroup((back_first,), group_count, (back_last,))
    spread_back = back_spread.reshape(inner_blocks, spread_width, token_count)
    returned_wide = returned.reshape(inner_blocks, spread_width, token_count)
    part_a = jnp.einsum("kit,kot->kio", inputs, spread_back, preferred_element_type=jnp.float32)
    part_b = jnp.einsum("qit,qjt->qij", permuted, back_hidden, preferred_element_type=jnp.float32)
    part_c = jnp.einsum("qit,qjt->qij", active, back_mid, preferred_element_type=jnp.float32)
    part_e = jnp.einsum("kot,kjt->koj", returned_wide, upstream, preferred_element_type=jnp.float32)
    grad_a, grad_b, grad_c, grad_e = (
        lax.psum_scatter(part_a.astype(jnp.bfloat16), "dp", scatter_dimension=1, tiled=True).astype(
            jnp.float32
        ),
        lax.psum_scatter(part_b.astype(jnp.bfloat16), "dp", scatter_dimension=1, tiled=True).astype(
            jnp.float32
        ),
        lax.psum_scatter(part_c.astype(jnp.bfloat16), "dp", scatter_dimension=1, tiled=True).astype(
            jnp.float32
        ),
        lax.psum_scatter(part_e.astype(jnp.bfloat16), "dp", scatter_dimension=1, tiled=True).astype(
            jnp.float32
        ),
    )
    output = output.astype(jnp.bfloat16).transpose(2, 0, 1).reshape(token_count, inner_blocks * BLK)
    grad_in = (
        back_input.astype(jnp.bfloat16).transpose(2, 0, 1).reshape(token_count, inner_blocks * BLK)
    )
    return (output, grad_in, grad_a, grad_b, grad_c, grad_e)


def solution(mesh):
    in_specs = (
        P("dp", "bfly"),
        P("dp", "bfly"),
        P("bfly", "dp", None),
        P("bfly", "dp", None),
        P("bfly", "dp", None),
        P("bfly", "dp", None),
    )
    out_specs = (
        P("dp", "bfly"),
        P("dp", "bfly"),
        P("bfly", "dp", None),
        P("bfly", "dp", None),
        P("bfly", "dp", None),
        P("bfly", "dp", None),
    )
    return jax.shard_map(
        per_device, mesh=mesh, in_specs=in_specs, out_specs=out_specs, check_vma=False
    )
```

profile of v0, /device:TPU:0, one launch (start us, length us, event | category | flops | bytes accessed | tf_op | source)
XLA Modules:
  0.0 599.6 jit_solution(6045464597825398712)
XLA Ops:
  11.7 61.7 %all-gather.5.cloned.1.call-done = bf16[12,256,512]{2,1,0:T(8,128)(2,1)} async-done(((bf16[12,32,512]{2,1,0:T(8,128)(2,1)}), bf16[12,256,512]{2,1,0:T(8,128)(2,1)}) %all-gather.5.cloned.1.call-update) | async-done | bytes 3145744 | tf_op jit(solution)/shard_map/all_gather | solution.py:37
  73.4 3.0 convolution_convert_fusion.2
  78.3 4.8 all-to-all-start
  83.9 50.9 %all-gather.11.cloned.1.call-done = bf16[12,512,256]{2,1,0:T(8,128)(2,1)} async-done(((bf16[12,64,256]{2,1,0:T(8,128)(2,1)}), bf16[12,512,256]{2,1,0:T(8,128)(2,1)}) %all-gather.11.cloned.1.call-update) | async-done | bytes 3145744 | tf_op jit(solution)/shard_map/all_gather | solution.py:40
  134.8 2.9 convolution_convert_fusion.1
  139.8 4.7 all-to-all-start.2
  146.6 34.8 %all-to-all-done.2 = bf16[1,24,4,64,256]{4,3,1,0,2:T(8,128)(2,1)} async-done(((bf16[1,24,4,64,256]{4,3,1,0,2:T(8,128)(2,1)}), bf16[1,24,4,64,256]{4,3,1,0,2:T(8,128)(2,1)}, u32[]{:S(2)}, u32[]{:S(2)}) %all-to-all-start.2) | async-done | bytes 3145760 | tf_op jit(solution)/shard_map/all_to_all | solution.py:27
  181.5 4.0 copy.45
  185.5 10.7 %all-gather.7.cloned.1.call-done = bf16[24,256,256]{2,1,0:T(8,128)(2,1)} async-done(((bf16[24,32,256]{2,1,0:T(8,128)(2,1)}), bf16[24,256,256]{2,1,0:T(8,128)(2,1)}) %all-gather.7.cloned.1.call-update) | async-done | bytes 3145744 | tf_op jit(solution)/shard_map/all_gather | solution.py:38
  196.1 5.6 fusion.7
  201.7 55.6 %all-gather.9.cloned.1.call-done = bf16[24,256,256]{2,1,0:T(8,128)(2,1)} async-done(((bf16[24,32,256]{2,1,0:T(8,128)(2,1)}), bf16[24,256,256]{2,1,0:T(8,128)(2,1)}) %all-gather.9.cloned.1.call-update) | async-done | bytes 3145744 | tf_op jit(solution)/shard_map/all_gather | solution.py:39
  257.4 8.4 %fusion.6 = bf16[24,256,256]{1,2,0:T(8,128)(2,1)S(1)} fusion(f32[24,256,256]{2,1,0:T(8,128)} %fusion.7, bf16[24,256,256]{2,1,0:T(8,128)(2,1)} %bitcast.79, bf16[24,256,256]{2,1,0:T(8,128)(2,1)} %all-gather.9.cloned.1.call-done), kind=kOutput, calls=%fused_computation.8 | convolution fusion | flops 835190784 | bytes 15728640 | tf_op jit(solution)/shard_map/qjt,qij->qit/dot_general | solution.py:62
  272.0 7.0 %convolution_convert_fusion.3 = bf16[24,256,256]{2,1,0:T(8,128)(2,1)} fusion(bf16[24,256,256]{2,1,0:T(8,128)(2,1)S(1)} %bitcast.80, f32[24,256,256]{2,1,0:T(8,128)} %fusion.7), kind=kOutput, calls=%fused_computation.15 | convolution fusion | flops 821035008 | bytes 12582912 | tf_op jit(solution)/shard_map/qit,qjt->qij/dot_general | solution.py:96
  280.8 2.9 convolution_convert_fusion.5
  284.2 39.5 %all_to_all.20 = bf16[1,24,4,64,256]{4,3,1,0,2:T(8,128)(2,1)S(1)} all-to-all(bf16[1,24,4,64,256]{4,3,1,0,2:T(8,128)(2,1)S(1)} %copy.48), channel_id=1, replica_groups=mesh['dp'=8,'bfly'=4] {'bfly'}, dimensions={2} | all-to-all | bytes 6291456 | tf_op jit(solution)/shard_map/all_to_all | solution.py:27
  325.0 2.7 convert_bitcast_fusion
  327.7 7.8 %copy.50 = bf16[12,256,512]{2,0,1:T(8,128)(2,1)} copy(bf16[12,256,512]{1,2,0:T(8,128)(2,1)} %convert_bitcast_fusion) | data formatting | bytes 6291456 | tf_op jit(solution)/shard_map/convert_element_type | solution.py:99
  335.6 6.6 %convolution_convert_fusion.6 = bf16[24,256,256]{1,2,0:T(8,128)(2,1)S(1)} fusion(bf16[24,256,256]{2,1,0:T(8,128)(2,1)} %all-gather.9.cloned.1.call-done, f32[24,256,256]{2,1,0:T(8,128)} %fusion.7), kind=kOutput, calls=%fused_computation.18 | convolution fusion | flops 821035008 | bytes 12582912 | tf_op jit(solution)/shard_map/qit,qij->qjt/dot_general | solution.py:82
  342.4 39.4 %all_to_all.21 = bf16[1,24,4,64,256]{4,3,1,0,2:T(8,128)(2,1)S(1)} all-to-all(bf16[1,24,4,64,256]{4,3,1,0,2:T(8,128)(2,1)S(1)} %copy.41), channel_id=1, replica_groups=mesh['dp'=8,'bfly'=4] {'bfly'}, dimensions={2} | all-to-all | bytes 6291456 | tf_op jit(solution)/shard_map/all_to_all | solution.py:27
  386.6 5.1 convolution_convert_fusion.8
  394.3 4.0 convolution_convert_fusion.7
  402.8 18.3 %reduce-scatter.9.cloned.1.call-done = bf16[24,32,256]{2,1,0:T(8,128)(2,1)} async-done(((bf16[24,256,256]{2,1,0:T(8,128)(2,1)}), bf16[24,32,256]{2,1,0:T(8,128)(2,1)}) %reduce-scatter.9.cloned.1.call-update) | async-done | bytes 393232 | tf_op jit(solution)/shard_map/reduce_scatter | solution.py:105
  423.1 88.9 %reduce-scatter.5.cloned.1.call-done = bf16[12,32,512]{2,0,1:T(8,128)(2,1)} async-done(((bf16[12,256,512]{2,0,1:T(8,128)(2,1)}), bf16[12,32,512]{2,0,1:T(8,128)(2,1)}) %reduce-scatter.5.cloned.1.call-update) | async-done | bytes 393232 | tf_op jit(solution)/shard_map/reduce_scatter | solution.py:99
  514.2 76.7 %reduce-scatter.11.cloned.1.call-done = bf16[12,64,256]{2,1,0:T(8,128)(2,1)} async-done(((bf16[12,512,256]{2,1,0:T(8,128)(2,1)}), bf16[12,64,256]{2,1,0:T(8,128)(2,1)}) %reduce-scatter.11.cloned.1.call-update) | async-done | bytes 393232 | tf_op jit(solution)/shard_map/reduce_scatter | solution.py:108
  (53 shorter events, 39.3 us)
Async XLA Ops:
  7.2 66.3 %all-gather.5.cloned.1.call-start = ((), (), s32[]{:S(2)}) async-start(), calls=%async_computation.8 | async-start | bytes 3538944 | tf_op jit(solution)/shard_map/all_gather | solution.py:37
  7.9 126.9 %all-gather.11.cloned.1.call-start = ((), (), s32[]{:S(2)}) async-start(), calls=%async_computation.11 | async-start | bytes 3538944 | tf_op jit(solution)/shard_map/all_gather | solution.py:40
  8.6 187.5 %all-gather.7.cloned.1.call-start = ((), (), s32[]{:S(2)}) async-start(), calls=%async_computation.9 | async-start | bytes 3538944 | tf_op jit(solution)/shard_map/all_gather | solution.py:38
  9.4 248.0 %all-gather.9.cloned.1.call-start = ((), (), s32[]{:S(2)}) async-start(), calls=%async_computation.10 | async-start | bytes 3538944 | tf_op jit(solution)/shard_map/all_gather | solution.py:39
  11.7 64.8 %copy-start.3 = (bf16[256,3072]{0,1:T(8,128)(2,1)}, bf16[256,3072]{0,1:T(8,128)(2,1)S(1)}, u32[]{:S(2)}) copy-start(bf16[256,3072]{0,1:T(8,128)(2,1)S(1)} %copy.36) | copy-start | bytes 4718596
  78.3 4.8 copy-start.8
  78.3 61.4 %all-to-all-start = ((bf16[1,24,4,64,256]{4,3,1,0,2:T(8,128)(2,1)}), bf16[1,24,4,64,256]{4,3,1,0,2:T(8,128)(2,1)}, u32[]{:S(2)}, u32[]{:S(2)}) async-start(bf16[1,24,4,64,256]{4,3,1,0,2:T(8,128)(2,1)} %copy.37), calls=%async_computation | async-start | bytes 6291456 | tf_op jit(solution)/shard_map/all_to_all | solution.py:27
  83.9 53.8 %copy-start.1 = (bf16[256,3072]{0,1:T(8,128)(2,1)}, bf16[256,3072]{0,1:T(8,128)(2,1)S(1)}, u32[]{:S(2)}) copy-start(bf16[256,3072]{0,1:T(8,128)(2,1)S(1)} %copy.43) | copy-start | bytes 4718596
  139.8 41.7 %all-to-all-start.2 = ((bf16[1,24,4,64,256]{4,3,1,0,2:T(8,128)(2,1)}), bf16[1,24,4,64,256]{4,3,1,0,2:T(8,128)(2,1)}, u32[]{:S(2)}, u32[]{:S(2)}) async-start(bf16[1,24,4,64,256]{4,3,1,0,2:T(8,128)(2,1)} %copy.44), calls=%async_computation.2 | async-start | bytes 6291456 | tf_op jit(solution)/shard_map/all_to_all | solution.py:27
  144.5 256.4 %reduce-scatter.7.cloned.1.call-start = ((), (), s32[]{:S(2)}) async-start(), calls=%async_computation.13 | async-start | bytes 3538944 | tf_op jit(solution)/shard_map/reduce_scatter | solution.py:102
  265.7 1.7 copy-start.6
  270.1 1.9 copy-start.7
  270.1 151.0 %reduce-scatter.9.cloned.1.call-start = ((), (), s32[]{:S(2)}) async-start(), calls=%async_computation.14 | async-start | bytes 3538944 | tf_op jit(solution)/shard_map/reduce_scatter | solution.py:105
  279.0 1.9 copy-start.5
  279.0 233.0 %reduce-scatter.5.cloned.1.call-start = ((), (), s32[]{:S(2)}) async-start(), calls=%async_computation.12 | async-start | bytes 4718592 | tf_op jit(solution)/shard_map/reduce_scatter | solution.py:99
  323.6 1.4 copy-start.4
  335.5 255.3 %reduce-scatter.11.cloned.1.call-start = ((), (), s32[]{:S(2)}) async-start(), calls=%async_computation.15 | async-start | bytes 3538944 | tf_op jit(solution)/shard_map/reduce_scatter | solution.py:108
  381.9 2.1 copy-start.2
  382.3 1.6 copy-start
Sparse Core Ops, SparseCore 0:
  10.2 63.2 all-gather.4
  75.6 59.1 all-gather.10
  137.0 59.1 all-gather.6
  198.2 59.1 all-gather.8
  270.2 73.3 reduce-scatter.6
  347.1 73.9 reduce-scatter.8
  424.8 87.2 reduce-scatter.4
  516.1 74.7 reduce-scatter.10
where the time goes:
time: 601 us; the launch traced here: 600 us
  waiting for transfers between devices  400 us (67%)
  blocking collectives  78.9 us (13%)
  matrix products  53.5 us (9%)
  local copies, waits for them, and re-layouts  36.8 us (6%)
  between operations  14.3 us (2%)
  starting transfers between devices  10 us (2%)
    reduce_scatter x1, waiting for transfers between devices, per_device(): lax.psum_scatter(part_a.astype(jnp.bfloat16), 'dp', scatter_dimension=1,...  88.9 us
    all_to_all x2, blocking collectives, regroup(): lax.all_to_all(stacked, 'bfly', split_axis=2, concat_axis=2, tiled=True)  78.9 us
    reduce_scatter x1, waiting for transfers between devices, per_device(): lax.psum_scatter(part_e.astype(jnp.bfloat16), 'dp', scatter_dimension=1,...  76.7 us
    all_gather x1, waiting for transfers between devices, per_device(): lax.all_gather(weight_a, 'dp', axis=1, tiled=True)  61.7 us
    all_gather x1, waiting for transfers between devices, per_device(): lax.all_gather(weight_c, 'dp', axis=1, tiled=True)  55.6 us
    all_gather x1, waiting for transfers between devices, per_device(): lax.all_gather(weight_e, 'dp', axis=1, tiled=True)  50.9 us
    all_to_all x2, waiting for transfers between devices, regroup(): lax.all_to_all(stacked, 'bfly', split_axis=2, concat_axis=2, tiled=True)  34.8 us
    reduce_scatter x1, waiting for transfers between devices, per_device(): lax.psum_scatter(part_c.astype(jnp.bfloat16), 'dp', scatter_dimension=1,...  18.3 us
  transfers between devices with their start and end apart: 10, of which 8 were waited for; matrix products, arithmetic and copies ran while one was open for 13% of the time, Pallas kernels for 0%

commit v1 on v0

--- a/solution.py
+++ b/solution.py
@@ -1,3 +1,4 @@
+import functools
 import jax
 import jax.numpy as jnp
 from jax import lax
@@ -5,6 +6,41 @@
 
 BLK = 256
 gelu_scale = 0.7978845608028654
+
+
+def find_the_widths(v0, axis_name, dim_k):
+    u_next, taken_in, latest = (
+        lax.axis_size(axis_name),
+        lax.axis_index(axis_name),
+        v0.shape[dim_k],
+    )
+    g_now = lax.dynamic_update_slice_in_dim(
+        jnp.zeros(
+            tuple((p * u_next if pp == dim_k else p for pp, p in enumerate(v0.shape))), v0.dtype
+        ),
+        v0,
+        taken_in * latest,
+        axis=dim_k,
+    )
+    upper = all_values = v0
+    for h in [*range(1, u_next // 2 + 1)]:
+        upper = lax.ppermute(
+            upper, axis_name, tuple(((pp, (pp + 1) % u_next) for pp in range(u_next)))
+        )
+        g_now = lax.dynamic_update_slice_in_dim(
+            g_now, upper, (taken_in - h) % u_next * latest, axis=dim_k
+        )
+        if 2 * h < u_next:
+            all_values = lax.ppermute(
+                all_values, axis_name, tuple(((pp, (pp - 1) % u_next) for pp in range(u_next)))
+            )
+            g_now = lax.dynamic_update_slice_in_dim(
+                g_now, all_values, (taken_in + h) % u_next * latest, axis=dim_k
+            )
+    return g_now
+
+
+mix_sources_all_up = functools.partial(find_the_widths, axis_name="dp", dim_k=1)
 
 
 def gelu_pair(hidden):
@@ -37,7 +73,7 @@
         lax.all_gather(weight_a, "dp", axis=1, tiled=True),
         lax.all_gather(weight_b, "dp", axis=1, tiled=True),
         lax.all_gather(weight_c, "dp", axis=1, tiled=True),
-        lax.all_gather(weight_e, "dp", axis=1, tiled=True),
+        mix_sources_all_up(weight_e),
     )
     token_count = tokens.shape[0]
     inner_blocks = full_a.shape[0]

time: 601 us -> 575 us (0.957)
  waiting for transfers between devices: 400 us -> 355 us
  starting transfers between devices: 10 us -> 28.9 us
    ppermute x0 -> x7, waiting for transfers between devices: none -> 63.9 us  [the longest x4 61.2 us: find_the_widths(): lax.ppermute(upper, axis_name, tuple(((pp, (pp + 1) % u_next) for pp in r...]
    all_gather x1, waiting for transfers between devices: 61.7 us -> 3.77 us  [per_device(): lax.all_gather(weight_a, 'dp', axis=1, tiled=True)]
    all_gather x1 -> x0, waiting for transfers between devices: 50.9 us -> none  [per_device(): lax.all_gather(weight_e, 'dp', axis=1, tiled=True)]
    all_to_all x2, waiting for transfers between devices: 34.8 us -> 60.6 us  [regroup(): lax.all_to_all(stacked, 'bfly', split_axis=2, concat_axis=2, tiled=True)]
    ppermute x0 -> x7, starting transfers between devices: none -> 19 us  [the longest x4 9.61 us: find_the_widths(): lax.ppermute(upper, axis_name, tuple(((pp, (pp + 1) % u_next) for pp in r...]
    all_gather x1, waiting for transfers between devices: 55.6 us -> 41.2 us  [per_device(): lax.all_gather(weight_c, 'dp', axis=1, tiled=True)]
    all_gather x1, waiting for transfers between devices: 10.7 us -> 0.02 us  [per_device(): lax.all_gather(weight_b, 'dp', axis=1, tiled=True)]
    unnamed x23 -> x31, local copies, waits for them, and re-layouts: 17.7 us -> 19.3 us
  transfers between devices with their start and end apart: 10 -> 16, of which waited for: 8 -> 12; matrix products, arithmetic and copies ran while one was open for 13% -> 13% of each run, Pallas kernels for 0% -> 0%
where the time goes in v1:
time: 575 us; the launch traced here: 573 us
  waiting for transfers between devices  355 us (62%)
  blocking collectives  78.9 us (14%)
  matrix products  51.6 us (9%)
  local copies, waits for them, and re-layouts  38.9 us (7%)
  starting transfers between devices  28.9 us (5%)
  between operations  14.6 us (3%)
  other arithmetic  5.85 us (1%)
    reduce_scatter x1, waiting for transfers between devices, per_device(): lax.psum_scatter(part_a.astype(jnp.bfloat16), 'dp', scatter_dimension=1,...  88.7 us
    all_to_all x2, blocking collectives, regroup(): lax.all_to_all(stacked, 'bfly', split_axis=2, concat_axis=2, tiled=True)  78.9 us
    reduce_scatter x1, waiting for transfers between devices, per_device(): lax.psum_scatter(part_e.astype(jnp.bfloat16), 'dp', scatter_dimension=1,...  76.7 us
    ppermute x4, waiting for transfers between devices, find_the_widths(): lax.ppermute(upper, axis_name, tuple(((pp, (pp + 1) % u_next) for pp in r...  61.2 us
    all_to_all x2, waiting for transfers between devices, regroup(): lax.all_to_all(stacked, 'bfly', split_axis=2, concat_axis=2, tiled=True)  60.6 us
    all_gather x1, waiting for transfers between devices, per_device(): lax.all_gather(weight_c, 'dp', axis=1, tiled=True)  41.2 us
    unnamed x31, local copies, waits for them, and re-layouts  19.3 us
    reduce_scatter x1, waiting for transfers between devices, per_device(): lax.psum_scatter(part_c.astype(jnp.bfloat16), 'dp', scatter_dimension=1,...  18.4 us
  transfers between devices with their start and end apart: 16, of which 12 were waited for; matrix products, arithmetic and copies ran while one was open for 13% of the time, Pallas kernels for 0%

profile of v1, /device:TPU:0, one launch (start us, length us, event | category | flops | bytes accessed | tf_op | source)
XLA Modules:
  0.0 573.5 jit_solution(5361612336812110299)
XLA Ops:
  14.8 18.2 %collective-permute-done = bf16[12,64,256]{2,1,0:T(8,128)(2,1)S(1)} collective-permute-done((bf16[12,64,256]{2,1,0:T(8,128)(2,1)}, bf16[12,64,256]{2,1,0:T(8,128)(2,1)S(1)}, u32[]{:S(2)}, u32[]{:S(2)}) %collective-permute-start) | collective-permute-done | bytes 393248 | tf_op jit(solution)/shard_map/ppermute | solution.py:27
  38.5 13.6 %collective-permute-done.2 = bf16[12,64,256]{2,1,0:T(8,128)(2,1)S(1)} collective-permute-done((bf16[12,64,256]{2,1,0:T(8,128)(2,1)S(1)}, bf16[12,64,256]{2,1,0:T(8,128)(2,1)S(1)}, u32[]{:S(2)}, u32[]{:S(2)}) %collective-permute-start.2) | collective-permute-done | bytes 393248 | tf_op jit(solution)/shard_map/ppermute | solution.py:27
  57.2 3.2 collective-permute-start.5
  60.4 18.9 %collective-permute-done.4 = bf16[12,64,256]{2,1,0:T(8,128)(2,1)S(1)} collective-permute-done((bf16[12,64,256]{2,1,0:T(8,128)(2,1)S(1)}, bf16[12,64,256]{2,1,0:T(8,128)(2,1)S(1)}, u32[]{:S(2)}, u32[]{:S(2)}) %collective-permute-start.4) | collective-permute-done | bytes 393248 | tf_op jit(solution)/shard_map/ppermute | solution.py:27
  84.6 10.5 %collective-permute-done.6 = bf16[12,64,256]{2,1,0:T(8,128)(2,1)S(1)} collective-permute-done((bf16[12,64,256]{2,1,0:T(8,128)(2,1)S(1)}, bf16[12,64,256]{2,1,0:T(8,128)(2,1)S(1)}, u32[]{:S(2)}, u32[]{:S(2)}) %collective-permute-start.6) | collective-permute-done | bytes 393248 | tf_op jit(solution)/shard_map/ppermute | solution.py:27
  98.9 4.8 all-to-all-start.2
  104.4 3.8 all-gather.4.cloned.1.call-done
  113.0 27.6 %all-to-all-done.2 = bf16[1,24,4,64,256]{4,3,1,0,2:T(8,128)(2,1)} async-done(((bf16[1,24,4,64,256]{4,3,1,0,2:T(8,128)(2,1)}), bf16[1,24,4,64,256]{4,3,1,0,2:T(8,128)(2,1)}, u32[]{:S(2)}, u32[]{:S(2)}) %all-to-all-start.2) | async-done | bytes 3145760 | tf_op jit(solution)/shard_map/all_to_all | solution.py:63
  140.7 4.6 all-to-all-start
  145.4 4.0 copy.48
  149.4 32.9 %all-to-all-done = bf16[1,24,4,64,256]{4,3,1,0,2:T(8,128)(2,1)} async-done(((bf16[1,24,4,64,256]{4,3,1,0,2:T(8,128)(2,1)}), bf16[1,24,4,64,256]{4,3,1,0,2:T(8,128)(2,1)}, u32[]{:S(2)}, u32[]{:S(2)}) %all-to-all-start) | async-done | bytes 3145760 | tf_op jit(solution)/shard_map/all_to_all | solution.py:63
  184.5 5.6 fusion.7
  190.0 41.2 %all-gather.8.cloned.1.call-done = bf16[24,256,256]{2,1,0:T(8,128)(2,1)} async-done(((bf16[24,32,256]{2,1,0:T(8,128)(2,1)}), bf16[24,256,256]{2,1,0:T(8,128)(2,1)}) %all-gather.8.cloned.1.call-update) | async-done | bytes 3145744 | tf_op jit(solution)/shard_map/all_gather | solution.py:75
  231.2 8.4 %fusion.6 = bf16[24,256,256]{1,2,0:T(8,128)(2,1)S(1)} fusion(f32[24,256,256]{2,1,0:T(8,128)} %fusion.7, bf16[24,256,256]{2,1,0:T(8,128)(2,1)} %bitcast.79, bf16[24,256,256]{2,1,0:T(8,128)(2,1)} %all-gather.8.cloned.1.call-done), kind=kOutput, calls=%fused_computation.8 | convolution fusion | flops 835190784 | bytes 15728640 | tf_op jit(solution)/shard_map/qjt,qij->qit/dot_general | solution.py:98
  245.9 7.0 %convolution_convert_fusion.3 = bf16[24,256,256]{2,1,0:T(8,128)(2,1)} fusion(bf16[24,256,256]{2,1,0:T(8,128)(2,1)S(1)} %bitcast.80, f32[24,256,256]{2,1,0:T(8,128)} %fusion.7), kind=kOutput, calls=%fused_computation.15 | convolution fusion | flops 821035008 | bytes 12582912 | tf_op jit(solution)/shard_map/qit,qjt->qij/dot_general | solution.py:132
  258.1 39.5 %all_to_all.20 = bf16[1,24,4,64,256]{4,3,1,0,2:T(8,128)(2,1)S(1)} all-to-all(bf16[1,24,4,64,256]{4,3,1,0,2:T(8,128)(2,1)S(1)} %copy.51), channel_id=1, replica_groups=mesh['dp'=8,'bfly'=4] {'bfly'}, dimensions={2} | all-to-all | bytes 6291456 | tf_op jit(solution)/shard_map/all_to_all | solution.py:63
  301.7 7.8 %copy.53 = bf16[12,256,512]{2,0,1:T(8,128)(2,1)} copy(bf16[12,256,512]{1,2,0:T(8,128)(2,1)} %convert_bitcast_fusion) | data formatting | bytes 6291456 | tf_op jit(solution)/shard_map/convert_element_type | solution.py:135
  309.5 6.6 %convolution_convert_fusion.6 = bf16[24,256,256]{1,2,0:T(8,128)(2,1)S(1)} fusion(bf16[24,256,256]{2,1,0:T(8,128)(2,1)} %all-gather.8.cloned.1.call-done, f32[24,256,256]{2,1,0:T(8,128)} %fusion.7), kind=kOutput, calls=%fused_computation.18 | convolution fusion | flops 821035008 | bytes 12582912 | tf_op jit(solution)/shard_map/qit,qij->qjt/dot_general | solution.py:118
  316.4 39.5 %all_to_all.21 = bf16[1,24,4,64,256]{4,3,1,0,2:T(8,128)(2,1)S(1)} all-to-all(bf16[1,24,4,64,256]{4,3,1,0,2:T(8,128)(2,1)S(1)} %copy.43), channel_id=1, replica_groups=mesh['dp'=8,'bfly'=4] {'bfly'}, dimensions={2} | all-to-all | bytes 6291456 | tf_op jit(solution)/shard_map/all_to_all | solution.py:63
  360.5 5.1 convolution_convert_fusion.8
  368.2 4.0 convolution_convert_fusion.7
  376.8 18.4 %reduce-scatter.9.cloned.1.call-done = bf16[24,32,256]{2,1,0:T(8,128)(2,1)} async-done(((bf16[24,256,256]{2,1,0:T(8,128)(2,1)}), bf16[24,32,256]{2,1,0:T(8,128)(2,1)}) %reduce-scatter.9.cloned.1.call-update) | async-done | bytes 393232 | tf_op jit(solution)/shard_map/reduce_scatter | solution.py:141
  397.1 88.7 %reduce-scatter.5.cloned.1.call-done = bf16[12,32,512]{2,0,1:T(8,128)(2,1)} async-done(((bf16[12,256,512]{2,0,1:T(8,128)(2,1)}), bf16[12,32,512]{2,0,1:T(8,128)(2,1)}) %reduce-scatter.5.cloned.1.call-update) | async-done | bytes 393232 | tf_op jit(solution)/shard_map/reduce_scatter | solution.py:135
  488.0 76.7 %reduce-scatter.11.cloned.1.call-done = bf16[12,64,256]{2,1,0:T(8,128)(2,1)} async-done(((bf16[12,512,256]{2,1,0:T(8,128)(2,1)}), bf16[12,64,256]{2,1,0:T(8,128)(2,1)}) %reduce-scatter.11.cloned.1.call-update) | async-done | bytes 393232 | tf_op jit(solution)/shard_map/reduce_scatter | solution.py:144
  (81 shorter events, 68.4 us)
Async XLA Ops:
  7.2 101.0 %all-gather.4.cloned.1.call-start = ((), (), s32[]{:S(2)}) async-start(), calls=%async_computation.8 | async-start | bytes 3538944 | tf_op jit(solution)/shard_map/all_gather | solution.py:73
  7.9 176.6 %all-gather.6.cloned.1.call-start = ((), (), s32[]{:S(2)}) async-start(), calls=%async_computation.9 | async-start | bytes 3538944 | tf_op jit(solution)/shard_map/all_gather | solution.py:74
  8.6 222.6 %all-gather.8.cloned.1.call-start = ((), (), s32[]{:S(2)}) async-start(), calls=%async_computation.10 | async-start | bytes 3538944 | tf_op jit(solution)/shard_map/all_gather | solution.py:75
  8.7 24.3 %collective-permute-start = (bf16[12,64,256]{2,1,0:T(8,128)(2,1)}, bf16[12,64,256]{2,1,0:T(8,128)(2,1)S(1)}, u32[]{:S(2)}, u32[]{:S(2)}) collective-permute-start(bf16[12,64,256]{2,1,0:T(8,128)(2,1)} %param.11), channel_id=1, source_target_pairs={{0,4},{4,8},{8,12},{12,16},{16,20},{20,24},{24,28},{28,0},{1,5},{5... | collective-permute-start | bytes 1179656 | tf_op jit(solution)/shard_map/ppermute | solution.py:27
  11.7 23.7 %collective-permute-start.1 = (bf16[12,64,256]{2,1,0:T(8,128)(2,1)}, bf16[12,64,256]{2,1,0:T(8,128)(2,1)S(1)}, u32[]{:S(2)}, u32[]{:S(2)}) collective-permute-start(bf16[12,64,256]{2,1,0:T(8,128)(2,1)} %param.11), channel_id=1, source_target_pairs={{0,28},{4,0},{8,4},{12,8},{16,12},{20,16},{24,20},{28,24},{1,29},{... | collective-permute-start | bytes 1179656 | tf_op jit(solution)/shard_map/ppermute | solution.py:34
  33.0 19.1 %copy-start.11 = (bf16[12,64,256]{2,1,0:T(8,128)(2,1)}, bf16[12,64,256]{2,1,0:T(8,128)(2,1)S(1)}, u32[]{:S(2)}) copy-start(bf16[12,64,256]{2,1,0:T(8,128)(2,1)S(1)} %collective-permute-done) | copy-start | bytes 1179652
  33.0 19.1 %collective-permute-start.2 = (bf16[12,64,256]{2,1,0:T(8,128)(2,1)S(1)}, bf16[12,64,256]{2,1,0:T(8,128)(2,1)S(1)}, u32[]{:S(2)}, u32[]{:S(2)}) collective-permute-start(bf16[12,64,256]{2,1,0:T(8,128)(2,1)S(1)} %collective-permute-done), channel_id=1, source_target_pairs={{0,4},{4,8},{8,12},{12,16},{16,20},{20,24},{24,28},{28,0},{1,5},{5... | collective-permute-start | bytes 1179656 | tf_op jit(solution)/shard_map/ppermute | solution.py:27
  35.4 21.8 %collective-permute-start.3 = (bf16[12,64,256]{2,1,0:T(8,128)(2,1)S(1)}, bf16[12,64,256]{2,1,0:T(8,128)(2,1)S(1)}, u32[]{:S(2)}, u32[]{:S(2)}) collective-permute-start(bf16[12,64,256]{2,1,0:T(8,128)(2,1)S(1)} %collective-permute-done.1), channel_id=1, source_target_pairs={{0,28},{4,0},{8,4},{12,8},{16,12},{20,16},{24,20},{28,24},{1,29},{... | collective-permute-start | bytes 1179656 | tf_op jit(solution)/shard_map/ppermute | solution.py:34
  52.1 27.1 %collective-permute-start.4 = (bf16[12,64,256]{2,1,0:T(8,128)(2,1)S(1)}, bf16[12,64,256]{2,1,0:T(8,128)(2,1)S(1)}, u32[]{:S(2)}, u32[]{:S(2)}) collective-permute-start(bf16[12,64,256]{2,1,0:T(8,128)(2,1)S(1)} %collective-permute-done.2), channel_id=1, source_target_pairs={{0,4},{4,8},{8,12},{12,16},{16,20},{20,24},{24,28},{28,0},{1,5},{5... | collective-permute-start | bytes 1179656 | tf_op jit(solution)/shard_map/ppermute | solution.py:27
  54.0 2.1 copy-start.10
  55.8 39.4 %copy-start.2 = (bf16[256,3072]{0,1:T(8,128)(2,1)}, bf16[256,3072]{0,1:T(8,128)(2,1)S(1)}, u32[]{:S(2)}) copy-start(bf16[256,3072]{0,1:T(8,128)(2,1)S(1)} %copy.46) | copy-start | bytes 4718596
  57.2 27.4 %collective-permute-start.5 = (bf16[12,64,256]{2,1,0:T(8,128)(2,1)S(1)}, bf16[12,64,256]{2,1,0:T(8,128)(2,1)S(1)}, u32[]{:S(2)}, u32[]{:S(2)}) collective-permute-start(bf16[12,64,256]{2,1,0:T(8,128)(2,1)S(1)} %collective-permute-done.3), channel_id=1, source_target_pairs={{0,28},{4,0},{8,4},{12,8},{16,12},{20,16},{24,20},{28,24},{1,29},{... | collective-permute-start | bytes 1179656 | tf_op jit(solution)/shard_map/ppermute | solution.py:34
  79.3 15.8 %collective-permute-start.6 = (bf16[12,64,256]{2,1,0:T(8,128)(2,1)S(1)}, bf16[12,64,256]{2,1,0:T(8,128)(2,1)S(1)}, u32[]{:S(2)}, u32[]{:S(2)}) collective-permute-start(bf16[12,64,256]{2,1,0:T(8,128)(2,1)S(1)} %collective-permute-done.4), channel_id=1, source_target_pairs={{0,4},{4,8},{8,12},{12,16},{16,20},{20,24},{24,28},{28,0},{1,5},{5... | collective-permute-start | bytes 1179656 | tf_op jit(solution)/shard_map/ppermute | solution.py:27
  98.9 4.8 copy-start.9
  98.9 41.8 %all-to-all-start.2 = ((bf16[1,24,4,64,256]{4,3,1,0,2:T(8,128)(2,1)}), bf16[1,24,4,64,256]{4,3,1,0,2:T(8,128)(2,1)}, u32[]{:S(2)}, u32[]{:S(2)}) async-start(bf16[1,24,4,64,256]{4,3,1,0,2:T(8,128)(2,1)} %copy.47), calls=%async_computation.2 | async-start | bytes 6291456 | tf_op jit(solution)/shard_map/all_to_all | solution.py:63
  104.4 6.8 %copy-start.4 = (bf16[256,3072]{0,1:T(8,128)(2,1)}, bf16[256,3072]{0,1:T(8,128)(2,1)S(1)}, u32[]{:S(2)}) copy-start(bf16[256,3072]{0,1:T(8,128)(2,1)S(1)} %copy.38) | copy-start | bytes 4718596
  140.7 41.6 %all-to-all-start = ((bf16[1,24,4,64,256]{4,3,1,0,2:T(8,128)(2,1)}), bf16[1,24,4,64,256]{4,3,1,0,2:T(8,128)(2,1)}, u32[]{:S(2)}, u32[]{:S(2)}) async-start(bf16[1,24,4,64,256]{4,3,1,0,2:T(8,128)(2,1)} %copy.39), calls=%async_computation | async-start | bytes 6291456 | tf_op jit(solution)/shard_map/all_to_all | solution.py:63
  145.3 229.5 %reduce-scatter.7.cloned.1.call-start = ((), (), s32[]{:S(2)}) async-start(), calls=%async_computation.12 | async-start | bytes 3538944 | tf_op jit(solution)/shard_map/reduce_scatter | solution.py:138
  244.0 1.9 copy-start.8
  244.0 151.2 %reduce-scatter.9.cloned.1.call-start = ((), (), s32[]{:S(2)}) async-start(), calls=%async_computation.13 | async-start | bytes 3538944 | tf_op jit(solution)/shard_map/reduce_scatter | solution.py:141
  252.9 1.9 copy-start.6
  252.9 232.9 %reduce-scatter.5.cloned.1.call-start = ((), (), s32[]{:S(2)}) async-start(), calls=%async_computation.11 | async-start | bytes 4718592 | tf_op jit(solution)/shard_map/reduce_scatter | solution.py:135
  309.5 255.2 %reduce-scatter.11.cloned.1.call-start = ((), (), s32[]{:S(2)}) async-start(), calls=%async_computation.14 | async-start | bytes 3538944 | tf_op jit(solution)/shard_map/reduce_scatter | solution.py:144
  355.8 2.1 copy-start.3
  (5 other events, 7.7 us)
Sparse Core Ops, SparseCore 0:
  10.2 97.9 all-gather.3
  110.3 59.4 all-gather.5
  172.1 59.1 all-gather.7
  244.1 73.5 reduce-scatter.6
  321.2 73.9 reduce-scatter.8
  398.7 87.1 reduce-scatter.4
  489.9 74.7 reduce-scatter.10
